TPU v7x, 32 devices: a whole 2x2x4 slice. The times are simulated.
32 devices in a mesh: groups: 2 (over y), arow: 16 (over z, x, core).
Axes of the slice: x: 2, y: 2, z: 4, core: 2. Of those that a mesh axis runs over, the one named last changes fastest.
Arguments:
- feat_a: bfloat16 [64, 32, 256], P(('groups', 'arow')), parts along dimension 0, may hold values from -6 to 6
- feat_b: bfloat16 [32, 32, 256], P(('groups', 'arow')), parts along dimension 0, may hold values from -6 to 6
- a_first: float32 [8, 3, 3], replicated, may hold values from -2 to 2
- b_first: float32 [8, 3, 3], replicated, may hold values from -2 to 2
- bias_first: float32 [8], replicated, may hold values from -3 to 3
- a_second: float32 [8, 3, 3], replicated, may hold values from -1.5 to 1.5
- b_second: float32 [8, 3, 3], replicated, may hold values from -1.5 to 1.5
- bias_second: float32 [1], replicated, may hold values from -3 to 3
Outputs:
- matches: float32 [64, 32, 512], P(('groups', 'arow')), parts along dimension 0
There are 2 independent parts, one for each index of `groups`. A program takes and returns all parts, laid end to end along the dimension named above; an argument that names none is the same for every part. Nothing has to cross between parts.
All inputs are finite; a program needn't handle non-finite values.
Results may differ from a plain program's by a relative error of at most 0.0081.
Values may be sent and summed in bfloat16 or wider, within the bound.
No kernel may reach another device: no remote copies, remote signals or barrier semaphores. Data moves between devices by JAX's collectives and lax.ppermute only.
A program may use at most 128 MiB of HBM per device.

v0:
```python
import jax
import jax.numpy as jnp
from jax import lax
from jax.sharding import PartitionSpec as P

EPSILON = 1e-05


def padded(cells, sides, width):
    for axis, dim in sides:
        count = lax.axis_size(axis)
        ends = count - 1
        head = lax.slice_in_dim(cells, 0, width, axis=dim)
        tail = lax.slice_in_dim(cells, cells.shape[dim] - width, cells.shape[dim], axis=dim)
        cells = jnp.concatenate(
            [
                lax.ppermute(tail, axis, [(i, (i + 1) % count) for i in range(ends)]),
                cells,
                lax.ppermute(head, axis, [((i + 1) % count, i) for i in range(ends)]),
            ],
            axis=dim,
        )
    return cells


def shifted_zero(values, along, offset):
    extent = values.shape[along]
    if offset == 0:
        return values
    widths = [(0, 0)] * values.ndim
    if offset > 0:
        widths[along] = (0, offset)
        return lax.slice_in_dim(jnp.pad(values, widths), offset, offset + extent, axis=along)
    widths[along] = (-offset, 0)
    return lax.slice_in_dim(jnp.pad(values, widths), 0, extent, axis=along)


def conv_a(values, kernel):
    out_rows = values.shape[-3] - 2
    result = 0.0
    for row_tap in range(3):
        row_slab = lax.slice_in_dim(
            values, row_tap, row_tap + out_rows, axis=values.ndim - 3
        ).astype(jnp.float32)
        for col_tap in range(3):
            result = result + kernel[..., row_tap, col_tap][..., None, None, None] * shifted_zero(
                row_slab, values.ndim - 2, col_tap - 1
            )
    return result


def conv_b(values, kernel, map_width):
    flat_pos = lax.broadcasted_iota(jnp.int32, (values.shape[-1],), 0) % map_width
    result = 0.0
    for row_tap in range(3):
        for col_tap in range(3):
            shifted = shifted_zero(
                values, values.ndim - 1, (row_tap - 1) * map_width + (col_tap - 1)
            )
            inside = ((flat_pos + col_tap - 1 >= 0) & (flat_pos + col_tap - 1 < map_width)).astype(
                jnp.float32
            )
            result = result + kernel[..., row_tap, col_tap][..., None, None, None] * (
                shifted * inside
            )
    return result


def first_layer(correlation, kern_a, kern_b, bias_one, map_width):
    spread = conv_a(correlation, kern_a)
    return jax.nn.relu(conv_b(spread, kern_b, map_width) + bias_one[:, None, None, None]).astype(
        jnp.bfloat16
    )


def second_layer(hidden, kern_a, kern_b, bias_two, map_width):
    spread = conv_a(hidden, kern_a)
    summed = jnp.sum(conv_b(spread, kern_b, map_width), axis=0)
    return jax.nn.relu(summed + bias_two[0])


def on_device(feat_a, feat_b, a_first, b_first, bias_first, a_second, b_second, bias_second):
    map_width = feat_b.shape[1]
    channels = feat_a.shape[2]
    b_cells = feat_b.shape[0] * lax.axis_size("arow") * map_width
    a_rows = feat_a.reshape(-1, channels)
    tile_product = lax.dot_general(
        a_rows,
        lax.all_gather(feat_b, "arow", axis=0, tiled=True).reshape(-1, channels),
        (((1,), (1,)), ((), ())),
        preferred_element_type=jnp.float32,
    )
    correlation = (
        (tile_product * channels ** (-0.5))
        .astype(jnp.bfloat16)
        .reshape(feat_a.shape[0], map_width, b_cells)
    )
    correlation = padded(correlation, (("arow", 0),), 1)

    def network(kern_a1, kern_b1, kern_a2, kern_b2):
        hidden = first_layer(correlation, kern_a1, kern_b1, bias_first, map_width)
        hidden = padded(hidden, (("arow", 1),), 1)
        return second_layer(hidden, kern_a2, kern_b2, bias_second, map_width)

    score = network(a_first, b_first, a_second, b_second)
    score = score + network(b_first, a_first, b_second, a_second)
    best_over_a = lax.pmax(jnp.max(score, axis=(0, 1)), "arow")
    best_over_b = jnp.max(score, axis=2)[..., None]
    return score * (score / (best_over_a + EPSILON)) * (score / (best_over_b + EPSILON))


def solution(mesh):
    return jax.shard_map(
        on_device,
        mesh=mesh,
        in_specs=(
            P(("groups", "arow"), None, None),
            P(("groups", "arow"), None, None),
            P(),
            P(),
            P(),
            P(),
            P(),
            P(),
        ),
        out_specs=P(("groups", "arow"), None, None),
        check_vma=False,
    )
```

profile of v0, /device:TPU:0, one launch (start us, length us, event | category | flops | bytes accessed | tf_op | source)
XLA Modules:
  0.0 88.3 jit_solution(9698802883479565245)
XLA Ops:
  0.0 0.0 copy-start
  0.0 0.0 copy-start.1
  0.0 0.0 copy-start.2
  0.0 0.0 copy-start.3
  0.0 24.2 %all_gather.3 = bf16[16,32,256]{2,1,0:T(8,128)(2,1)S(1)} all-gather(bf16[1,32,256]{2,1,0:T(8,128)(2,1)} %param.9), channel_id=1, replica_groups=mesh['groups'=2,'arow'=16] {'arow'}, dimensions={0}, use_global_device_ids=true | all-gather | bytes 278528 | tf_op jit(solution)/shard_map/all_gather | solution.py:89
  24.2 0.0 copy-done
  24.2 0.2 fusion
  24.4 2.3 %collective-permute-start = (bf16[1,32,512]{2,1,0:T(8,128)(2,1)S(1)}, bf16[1,32,512]{2,1,0:T(8,128)(2,1)S(1)}, u32[]{:S(2)}, u32[]{:S(2)}) collective-permute-start(bf16[1,32,512]{2,1,0:T(8,128)(2,1)S(1)} %get-tuple-element.28), channel_id=1, source_target_pairs={{0,1},{1,2},{2,3},{3,4},{4,5},{5,6},{6,7},{7,8},{8,9},{9,10},{10,1... | collective-permute-start | bytes 98312 | tf_op jit(solution)/shard_map/ppermute | solution.py:17
  26.7 1.3 %collective-permute-start.1 = (bf16[1,32,512]{2,1,0:T(8,128)(2,1)S(1)}, bf16[1,32,512]{2,1,0:T(8,128)(2,1)S(1)}, u32[]{:S(2)}, u32[]{:S(2)}) collective-permute-start(bf16[1,32,512]{2,1,0:T(8,128)(2,1)S(1)} %get-tuple-element.29), channel_id=1, source_target_pairs={{1,0},{2,1},{3,2},{4,3},{5,4},{6,5},{7,6},{8,7},{9,8},{10,9},{11,1... | collective-permute-start | bytes 98312 | tf_op jit(solution)/shard_map/ppermute | solution.py:19
  28.0 0.8 slice_bitcast_fusion.34
  28.9 0.0 copy-done.1
  28.9 0.0 copy-done.2
  28.9 0.0 copy-done.3
  29.6 0.0 collective-permute-done
  29.6 0.1 collective-permute-done.1
  29.8 0.1 pad_slice_fusion.45
  29.8 0.7 multiply_add_fusion.1
  30.6 0.0 copy-start.4
  30.6 0.7 multiply_add_fusion
  31.3 0.0 copy-done.4
  31.3 2.5 %fusion.150 = (f32[8,2,32,512]{3,2,1,0:T(8,128)S(1)}, bf16[8,2,32,512]{3,2,1,0:T(8,128)(2,1)S(1)}) fusion(f32[8]{0:T(128)S(1)} %copy-done.4, f32[8,2,32,512]{3,2,1,0:T(8,128)S(1)} %multiply_add_fusion.1, f32[8]{0:T(128)S(1)} %get-tuple-element.64, f32[8]{0:T(128)S(1)} %get-tuple-element.65, f32[8]{0:T(128)S(1)} %get-tuple-element.58, ...), kind=kLoop, calls=%fused_computation.255 | loop fusion | flops 7864320 | bytes 2627904 | tf_op jit(solution)/shard_map/convert_element_type | solution.py:44
  33.8 4.1 %collective-permute-start.2 = (bf16[8,1,32,512]{3,2,1,0:T(8,128)(2,1)S(1)}, bf16[8,1,32,512]{3,2,1,0:T(8,128)(2,1)S(1)}, u32[]{:S(2)}, u32[]{:S(2)}) collective-permute-start(bf16[8,1,32,512]{3,2,1,0:T(8,128)(2,1)S(1)} %get-tuple-element.15), channel_id=1, source_target_pairs={{0,1},{1,2},{2,3},{3,4},{4,5},{5,6},{6,7},{7,8},{8,9},{9,10},{10,1... | collective-permute-start | bytes 786440 | tf_op jit(solution)/shard_map/ppermute | solution.py:17
  37.9 1.3 %collective-permute-start.3 = (bf16[8,1,32,512]{3,2,1,0:T(8,128)(2,1)S(1)}, bf16[8,1,32,512]{3,2,1,0:T(8,128)(2,1)S(1)}, u32[]{:S(2)}, u32[]{:S(2)}) collective-permute-start(bf16[8,1,32,512]{3,2,1,0:T(8,128)(2,1)S(1)} %get-tuple-element.14), channel_id=1, source_target_pairs={{1,0},{2,1},{3,2},{4,3},{5,4},{6,5},{7,6},{8,7},{9,8},{10,9},{11,1... | collective-permute-start | bytes 786440 | tf_op jit(solution)/shard_map/ppermute | solution.py:19
  39.2 2.5 %fusion.152 = (f32[8,2,32,512]{3,2,1,0:T(8,128)S(1)}, bf16[8,2,32,512]{3,2,1,0:T(8,128)(2,1)S(1)}) fusion(f32[8]{0:T(128)S(1)} %copy-done.4, f32[8,2,32,512]{3,2,1,0:T(8,128)S(1)} %multiply_add_fusion, f32[8]{0:T(128)S(1)} %get-tuple-element.55, f32[8]{0:T(128)S(1)} %get-tuple-element.56, f32[8]{0:T(128)S(1)} %get-tuple-element.49, ...), kind=kLoop, calls=%fused_computation.256 | loop fusion | flops 7864320 | bytes 2627904 | tf_op jit(solution)/shard_map/convert_element_type | solution.py:44
  41.7 3.0 %collective-permute-start.4 = (bf16[8,1,32,512]{3,2,1,0:T(8,128)(2,1)S(1)}, bf16[8,1,32,512]{3,2,1,0:T(8,128)(2,1)S(1)}, u32[]{:S(2)}, u32[]{:S(2)}) collective-permute-start(bf16[8,1,32,512]{3,2,1,0:T(8,128)(2,1)S(1)} %get-tuple-element.19), channel_id=1, source_target_pairs={{0,1},{1,2},{2,3},{3,4},{4,5},{5,6},{6,7},{7,8},{8,9},{9,10},{10,1... | collective-permute-start | bytes 786440 | tf_op jit(solution)/shard_map/ppermute | solution.py:17
  44.8 1.3 %collective-permute-start.5 = (bf16[8,1,32,512]{3,2,1,0:T(8,128)(2,1)S(1)}, bf16[8,1,32,512]{3,2,1,0:T(8,128)(2,1)S(1)}, u32[]{:S(2)}, u32[]{:S(2)}) collective-permute-start(bf16[8,1,32,512]{3,2,1,0:T(8,128)(2,1)S(1)} %get-tuple-element.18), channel_id=1, source_target_pairs={{1,0},{2,1},{3,2},{4,3},{5,4},{6,5},{7,6},{8,7},{9,8},{10,9},{11,1... | collective-permute-start | bytes 786440 | tf_op jit(solution)/shard_map/ppermute | solution.py:19
  46.1 0.0 collective-permute-done.2
  46.1 0.0 collective-permute-done.3
  46.1 0.1 fusion.135
  46.2 1.6 %fusion.35 = f32[8,2,32,512]{3,2,1,0:T(8,128)S(1)} fusion(f32[8,2,32,512]{3,2,1,0:T(8,128)S(1)} %get-tuple-element.13, f32[8,2,32,512]{3,2,1,0:T(8,128)S(1)} %get-tuple-element.8, f32[8,2,32,512]{3,2,1,0:T(8,128)S(1)} %get-tuple-element.12, f32[8]{0:T(128)S(1)} %get-tuple-element.37, f32[8]{0:T(128)S(1)} %get-tuple-element.38, f32[8]{0:T(128)S(1)} %get-tuple-element.31, ...), kind=kLoop, calls=%fused_computation.80 | loop fusion | flops 4456448 | bytes 4194592 | tf_op jit(solution)/shard_map/add | solution.py:46
  47.8 2.4 %fusion.132 = f32[2,32,512]{2,1,0:T(8,128)S(1)} fusion(f32[8,2,32,512]{3,2,1,0:T(8,128)S(1)} %fusion.35, f32[8]{0:T(128)S(1)} %get-tuple-element.46, f32[8]{0:T(128)S(1)} %get-tuple-element.47, f32[8]{0:T(128)S(1)} %get-tuple-element.40, f32[8]{0:T(128)S(1)} %get-tuple-element.41, f32[8]{0:T(128)S(1)} %get-tuple-element.42, f32[8]{0:T(128)S(1)} %get-tuple-element.43, ...), kind=kLoop, calls=%fused_computation.179 | loop fusion | flops 7045120 | bytes 1186080 | tf_op jit(solution)/shard_map/reduce_sum | solution.py:78
  50.3 0.0 collective-permute-done.4
  50.3 0.0 collective-permute-done.5
  50.3 0.1 fusion.133
  50.4 1.6 %fusion.99 = f32[8,2,32,512]{3,2,1,0:T(8,128)S(1)} fusion(f32[8,2,32,512]{3,2,1,0:T(8,128)S(1)} %get-tuple-element.17, f32[8,2,32,512]{3,2,1,0:T(8,128)S(1)} %get-tuple-element.10, f32[8,2,32,512]{3,2,1,0:T(8,128)S(1)} %get-tuple-element.16, f32[8]{0:T(128)S(1)} %get-tuple-element.46, f32[8]{0:T(128)S(1)} %get-tuple-element.47, f32[8]{0:T(128)S(1)} %get-tuple-element.40, ...), kind=kLoop, calls=%fused_computation.144 | loop fusion | flops 4456448 | bytes 4194592 | tf_op jit(solution)/shard_map/add | solution.py:46
  52.1 2.4 %fusion.131 = f32[2,32,512]{2,1,0:T(8,128)S(1)} fusion(f32[8,2,32,512]{3,2,1,0:T(8,128)S(1)} %fusion.99, f32[8]{0:T(128)S(1)} %get-tuple-element.37, f32[8]{0:T(128)S(1)} %get-tuple-element.38, f32[8]{0:T(128)S(1)} %get-tuple-element.31, f32[8]{0:T(128)S(1)} %get-tuple-element.32, f32[8]{0:T(128)S(1)} %get-tuple-element.33, f32[8]{0:T(128)S(1)} %get-tuple-element.34, ...), kind=kLoop, calls=%fused_computation.178 | loop fusion | flops 7045120 | bytes 1186080 | tf_op jit(solution)/shard_map/reduce_sum | solution.py:78
  54.5 0.1 fusion.149
  54.6 32.9 %pmax.7 = f32[512]{0:T(512)S(1)} all-reduce(f32[512]{0:T(512)S(1)} %get-tuple-element.5), channel_id=1, replica_groups=mesh['groups'=2,'arow'=16] {'arow'}, use_global_device_ids=true, to_apply=%region_3.4 | all-reduce | flops 512 | bytes 4096 | tf_op jit(solution)/shard_map/pmax | solution.py:107
  87.5 0.7 fusion.137
  (13 shorter events, 0.2 us)
Async XLA Ops:
  0.0 24.2 %copy-start = (bf16[2,32,256]{2,1,0:T(8,128)(2,1)S(1)}, bf16[2,32,256]{2,1,0:T(8,128)(2,1)}, u32[]{:S(2)}) copy-start(bf16[2,32,256]{2,1,0:T(8,128)(2,1)} %param.8) | copy-start | bytes 98308
  0.0 28.9 %copy-start.1 = (f32[8,3,3]{0,2,1:T(4,128)S(1)}, f32[8,3,3]{0,2,1:T(4,128)}, u32[]{:S(2)}) copy-start(f32[8,3,3]{0,2,1:T(4,128)} %param.11) | copy-start | bytes 868
  0.0 28.9 %copy-start.2 = (f32[8,3,3]{0,2,1:T(4,128)S(1)}, f32[8,3,3]{0,2,1:T(4,128)}, u32[]{:S(2)}) copy-start(f32[8,3,3]{0,2,1:T(4,128)} %param.13) | copy-start | bytes 868
  0.0 28.9 %copy-start.3 = (f32[8,3,3]{0,2,1:T(4,128)S(1)}, f32[8,3,3]{0,2,1:T(4,128)}, u32[]{:S(2)}) copy-start(f32[8,3,3]{0,2,1:T(4,128)} %param.14) | copy-start | bytes 868
  24.4 5.2 %collective-permute-start = (bf16[1,32,512]{2,1,0:T(8,128)(2,1)S(1)}, bf16[1,32,512]{2,1,0:T(8,128)(2,1)S(1)}, u32[]{:S(2)}, u32[]{:S(2)}) collective-permute-start(bf16[1,32,512]{2,1,0:T(8,128)(2,1)S(1)} %get-tuple-element.28), channel_id=1, source_target_pairs={{0,1},{1,2},{2,3},{3,4},{4,5},{5,6},{6,7},{7,8},{8,9},{9,10},{10,1... | collective-permute-start | bytes 98312 | tf_op jit(solution)/shard_map/ppermute | solution.py:17
  26.7 3.1 %collective-permute-start.1 = (bf16[1,32,512]{2,1,0:T(8,128)(2,1)S(1)}, bf16[1,32,512]{2,1,0:T(8,128)(2,1)S(1)}, u32[]{:S(2)}, u32[]{:S(2)}) collective-permute-start(bf16[1,32,512]{2,1,0:T(8,128)(2,1)S(1)} %get-tuple-element.29), channel_id=1, source_target_pairs={{1,0},{2,1},{3,2},{4,3},{5,4},{6,5},{7,6},{8,7},{9,8},{10,9},{11,1... | collective-permute-start | bytes 98312 | tf_op jit(solution)/shard_map/ppermute | solution.py:19
  30.6 0.7 copy-start.4
  33.8 12.2 %collective-permute-start.2 = (bf16[8,1,32,512]{3,2,1,0:T(8,128)(2,1)S(1)}, bf16[8,1,32,512]{3,2,1,0:T(8,128)(2,1)S(1)}, u32[]{:S(2)}, u32[]{:S(2)}) collective-permute-start(bf16[8,1,32,512]{3,2,1,0:T(8,128)(2,1)S(1)} %get-tuple-element.15), channel_id=1, source_target_pairs={{0,1},{1,2},{2,3},{3,4},{4,5},{5,6},{6,7},{7,8},{8,9},{9,10},{10,1... | collective-permute-start | bytes 786440 | tf_op jit(solution)/shard_map/ppermute | solution.py:17
  37.9 8.2 %collective-permute-start.3 = (bf16[8,1,32,512]{3,2,1,0:T(8,128)(2,1)S(1)}, bf16[8,1,32,512]{3,2,1,0:T(8,128)(2,1)S(1)}, u32[]{:S(2)}, u32[]{:S(2)}) collective-permute-start(bf16[8,1,32,512]{3,2,1,0:T(8,128)(2,1)S(1)} %get-tuple-element.14), channel_id=1, source_target_pairs={{1,0},{2,1},{3,2},{4,3},{5,4},{6,5},{7,6},{8,7},{9,8},{10,9},{11,1... | collective-permute-start | bytes 786440 | tf_op jit(solution)/shard_map/ppermute | solution.py:19
  41.7 8.6 %collective-permute-start.4 = (bf16[8,1,32,512]{3,2,1,0:T(8,128)(2,1)S(1)}, bf16[8,1,32,512]{3,2,1,0:T(8,128)(2,1)S(1)}, u32[]{:S(2)}, u32[]{:S(2)}) collective-permute-start(bf16[8,1,32,512]{3,2,1,0:T(8,128)(2,1)S(1)} %get-tuple-element.19), channel_id=1, source_target_pairs={{0,1},{1,2},{2,3},{3,4},{4,5},{5,6},{6,7},{7,8},{8,9},{9,10},{10,1... | collective-permute-start | bytes 786440 | tf_op jit(solution)/shard_map/ppermute | solution.py:17
  44.8 5.5 %collective-permute-start.5 = (bf16[8,1,32,512]{3,2,1,0:T(8,128)(2,1)S(1)}, bf16[8,1,32,512]{3,2,1,0:T(8,128)(2,1)S(1)}, u32[]{:S(2)}, u32[]{:S(2)}) collective-permute-start(bf16[8,1,32,512]{3,2,1,0:T(8,128)(2,1)S(1)} %get-tuple-element.18), channel_id=1, source_target_pairs={{1,0},{2,1},{3,2},{4,3},{5,4},{6,5},{7,6},{8,7},{9,8},{10,9},{11,1... | collective-permute-start | bytes 786440 | tf_op jit(solution)/shard_map/ppermute | solution.py:19
where the time goes:
time: 88.6 us; the launch traced here: 88.3 us
  blocking collectives  57.1 us (64%)
  other arithmetic  15.6 us (18%)
  starting transfers between devices  13.2 us (15%)
  local copies, waits for them, and re-layouts  1.06 us (1%)
  between operations  0.94 us (1%)
    pmax x1, blocking collectives, on_device(): best_over_a = lax.pmax(jnp.max(score, axis=(0, 1)), 'arow')  32.9 us
    all_gather x1, blocking collectives, on_device(): lax.all_gather(feat_b, 'arow', axis=0, tiled=True).reshape(-1, channels)  24.2 us
    ppermute x3, starting transfers between devices, padded(): lax.ppermute(tail, axis, [(i, (i + 1) % count) for i in range(ends)])  9.37 us
    convert_element_type x6, other arithmetic, conv_a(): row_slab = lax.slice_in_dim(values, row_tap, row_tap + out_rows, axis=val...  5.23 us
    reduce_sum x2, other arithmetic, second_layer(): summed = jnp.sum(conv_b(spread, kern_b, map_width), axis=0)  4.84 us
    add x4, other arithmetic, conv_a(): result + kernel[..., row_tap, col_tap][..., None, None, None] * shifted_z...  4.64 us
    ppermute x3, starting transfers between devices, padded(): lax.ppermute(head, axis, [((i + 1) % count, i) for i in range(ends)])  3.88 us
  transfers between devices with their start and end apart: 6, of which 1 were waited for; matrix products, arithmetic and copies ran while one was open for 9% of the time, Pallas kernels for 0%

commit v1 on v0

--- a/solution.py
+++ b/solution.py
@@ -4,6 +4,28 @@
 from jax.sharding import PartitionSpec as P
 
 EPSILON = 1e-05
+
+
+def joined_along(parts, dim):
+    shape = list(parts.shape[1:])
+    shape[dim] *= parts.shape[0]
+    return jnp.moveaxis(parts, 0, dim).reshape(shape)
+
+
+def ring_gather(array, axis, dim):
+    size = lax.axis_size(axis)
+    pairs = [(i, (i + 1) % size) for i in range(size)]
+    back = [(b, a) for a, b in pairs]
+    lower, upper = ([], [])
+    for step in range(size - 1):
+        if step % 2 == 0:
+            lower.append(lax.ppermute(lower[-1] if lower else array, axis, pairs))
+        else:
+            upper.append(lax.ppermute(upper[-1] if upper else array, axis, back))
+    blocks = jnp.stack([*lower[::-1], array, *upper])
+    shift = lax.axis_index(axis) - len(lower)
+    blocks = blocks[(jnp.arange(size) - shift) % size]
+    return joined_along(blocks, dim)
 
 
 def padded(cells, sides, width):
@@ -86,7 +108,7 @@
     a_rows = feat_a.reshape(-1, channels)
     tile_product = lax.dot_general(
         a_rows,
-        lax.all_gather(feat_b, "arow", axis=0, tiled=True).reshape(-1, channels),
+        ring_gather(feat_b, "arow", 0).reshape(-1, channels),
         (((1,), (1,)), ((), ())),
         preferred_element_type=jnp.float32,
     )

time: 88.6 us -> 116 us (1.31)
  starting transfers between devices: 13.2 us -> 42.5 us
  blocking collectives: 57.1 us -> 37.1 us
  waiting for transfers between devices: 0.15 us -> 13.8 us
  local copies, waits for them, and re-layouts: 1.06 us -> 4.87 us
    ppermute x0 -> x15, starting transfers between devices: none -> 32.1 us  [the longest x7 31.6 us: ring_gather(): upper.append(lax.ppermute(upper[-1] if upper else array, axis, back))]
    all_gather x1 -> x0, blocking collectives: 24.2 us -> none  [on_device(): lax.all_gather(feat_b, 'arow', axis=0, tiled=True).reshape(-1, channels)]
    ppermute x0 -> x15, waiting for transfers between devices: none -> 12 us  [the longest x8 8.8 us: ring_gather(): lower.append(lax.ppermute(lower[-1] if lower else array, axis, pairs))]
    pmax x1, blocking collectives: 32.9 us -> 37.1 us  [on_device(): best_over_a = lax.pmax(jnp.max(score, axis=(0, 1)), 'arow')]
    ppermute x3, starting transfers between devices: 9.37 us -> 6.42 us  [padded(): lax.ppermute(tail, axis, [(i, (i + 1) % count) for i in range(ends)])]
    mul x2, local copies, waits for them, and re-layouts: 0.01 us -> 1.69 us  [conv_b(): kernel[..., row_tap, col_tap][..., None, None, None] * (shifted * inside)]
    ppermute x3, waiting for transfers between devices: 0.15 us -> 1.75 us  [padded(): lax.ppermute(head, axis, [((i + 1) % count, i) for i in range(ends)])]
  transfers between devices with their start and end apart: 6 -> 21, of which waited for: 1 -> 15; matrix products, arithmetic and copies ran while one was open for 9% -> 9% of each run, Pallas kernels for 0% -> 0%
where the time goes in v1:
time: 116 us; the launch traced here: 115 us
  starting transfers between devices  42.5 us (37%)
  blocking collectives  37.1 us (32%)
  other arithmetic  15.6 us (13%)
  waiting for transfers between devices  13.8 us (12%)
  local copies, waits for them, and re-layouts  4.87 us (4%)
    pmax x1, blocking collectives, on_device(): best_over_a = lax.pmax(jnp.max(score, axis=(0, 1)), 'arow')  37.1 us
    ppermute x7, starting transfers between devices, ring_gather(): upper.append(lax.ppermute(upper[-1] if upper else array, axis, back))  31.6 us
    ppermute x8, waiting for transfers between devices, ring_gather(): lower.append(lax.ppermute(lower[-1] if lower else array, axis, pairs))  8.8 us
    ppermute x3, starting transfers between devices, padded(): lax.ppermute(tail, axis, [(i, (i + 1) % count) for i in range(ends)])  6.42 us
    convert_element_type x6, other arithmetic, conv_a(): row_slab = lax.slice_in_dim(values, row_tap, row_tap + out_rows, axis=val...  5.23 us
    reduce_sum x2, other arithmetic, second_layer(): summed = jnp.sum(conv_b(spread, kern_b, map_width), axis=0)  4.84 us
    add x4, other arithmetic, conv_a(): result + kernel[..., row_tap, col_tap][..., None, None, None] * shifted_z...  4.64 us
    ppermute x3, starting transfers between devices, padded(): lax.ppermute(head, axis, [((i + 1) % count, i) for i in range(ends)])  4.06 us
  transfers between devices with their start and end apart: 21, of which 15 were waited for; matrix products, arithmetic and copies ran while one was open for 9% of the time, Pallas kernels for 0%

profile of v1, /device:TPU:0, one launch (start us, length us, event | category | flops | bytes accessed | tf_op | source)
XLA Modules:
  0.0 115.1 jit_solution(9090903741477587028)
XLA Ops:
  0.0 0.5 collective-permute-start
  0.5 5.0 %collective-permute-start.8 = (bf16[1,32,256]{2,1,0:T(8,128)(2,1)}, bf16[1,32,256]{2,1,0:T(8,128)(2,1)S(1)}, u32[]{:S(2)}, u32[]{:S(2)}) collective-permute-start(bf16[1,32,256]{2,1,0:T(8,128)(2,1)} %param.9), channel_id=1, source_target_pairs={{1,0},{2,1},{3,2},{4,3},{5,4},{6,5},{7,6},{8,7},{9,8},{10,9},{11,1... | collective-permute-start | bytes 49160 | tf_op jit(solution)/shard_map/ppermute | solution.py:24
  5.5 0.8 slice_bitcast_fusion.34
  6.3 0.7 collective-permute-done
  7.1 0.0 collective-permute-start.1
  7.1 0.8 slice_bitcast_fusion.35
  7.9 5.0 %collective-permute-done.1 = bf16[1,32,256]{2,1,0:T(8,128)(2,1)S(1)} collective-permute-done((bf16[1,32,256]{2,1,0:T(8,128)(2,1)S(1)}, bf16[1,32,256]{2,1,0:T(8,128)(2,1)S(1)}, u32[]{:S(2)}, u32[]{:S(2)}) %collective-permute-start.1) | collective-permute-done | bytes 16416 | tf_op jit(solution)/shard_map/ppermute | solution.py:22
  12.9 0.0 collective-permute-start.2
  12.9 0.8 slice_bitcast_fusion.36
  13.8 0.0 collective-permute-done.8
  13.8 4.5 %collective-permute-start.9 = (bf16[1,32,256]{2,1,0:T(8,128)(2,1)S(1)}, bf16[1,32,256]{2,1,0:T(8,128)(2,1)S(1)}, u32[]{:S(2)}, u32[]{:S(2)}) collective-permute-start(bf16[1,32,256]{2,1,0:T(8,128)(2,1)S(1)} %collective-permute-done.8), channel_id=1, source_target_pairs={{1,0},{2,1},{3,2},{4,3},{5,4},{6,5},{7,6},{8,7},{9,8},{10,9},{11,1... | collective-permute-start | bytes 49160 | tf_op jit(solution)/shard_map/ppermute | solution.py:24
  18.3 0.5 collective-permute-done.2
  18.8 0.0 collective-permute-start.3
  18.8 0.8 slice_bitcast_fusion.37
  19.6 0.1 collective-permute-done.9
  19.7 4.4 %collective-permute-start.10 = (bf16[1,32,256]{2,1,0:T(8,128)(2,1)S(1)}, bf16[1,32,256]{2,1,0:T(8,128)(2,1)S(1)}, u32[]{:S(2)}, u32[]{:S(2)}) collective-permute-start(bf16[1,32,256]{2,1,0:T(8,128)(2,1)S(1)} %collective-permute-done.9), channel_id=1, source_target_pairs={{1,0},{2,1},{3,2},{4,3},{5,4},{6,5},{7,6},{8,7},{9,8},{10,9},{11,1... | collective-permute-start | bytes 49160 | tf_op jit(solution)/shard_map/ppermute | solution.py:24
  24.1 0.5 collective-permute-done.3
  24.6 0.0 collective-permute-start.4
  24.7 0.9 collective-permute-done.10
  25.6 4.4 %collective-permute-start.11 = (bf16[1,32,256]{2,1,0:T(8,128)(2,1)S(1)}, bf16[1,32,256]{2,1,0:T(8,128)(2,1)S(1)}, u32[]{:S(2)}, u32[]{:S(2)}) collective-permute-start(bf16[1,32,256]{2,1,0:T(8,128)(2,1)S(1)} %collective-permute-done.10), channel_id=1, source_target_pairs={{1,0},{2,1},{3,2},{4,3},{5,4},{6,5},{7,6},{8,7},{9,8},{10,9},{11,1... | collective-permute-start | bytes 49160 | tf_op jit(solution)/shard_map/ppermute | solution.py:24
  30.0 0.5 collective-permute-done.4
  30.5 0.0 collective-permute-start.5
  30.5 0.9 collective-permute-done.11
  31.4 4.4 %collective-permute-start.12 = (bf16[1,32,256]{2,1,0:T(8,128)(2,1)S(1)}, bf16[1,32,256]{2,1,0:T(8,128)(2,1)S(1)}, u32[]{:S(2)}, u32[]{:S(2)}) collective-permute-start(bf16[1,32,256]{2,1,0:T(8,128)(2,1)S(1)} %collective-permute-done.11), channel_id=1, source_target_pairs={{1,0},{2,1},{3,2},{4,3},{5,4},{6,5},{7,6},{8,7},{9,8},{10,9},{11,1... | collective-permute-start | bytes 49160 | tf_op jit(solution)/shard_map/ppermute | solution.py:24
  35.8 0.5 collective-permute-done.5
  36.4 0.0 collective-permute-start.6
  36.4 0.9 collective-permute-done.12
  37.3 4.4 %collective-permute-start.13 = (bf16[1,32,256]{2,1,0:T(8,128)(2,1)S(1)}, bf16[1,32,256]{2,1,0:T(8,128)(2,1)S(1)}, u32[]{:S(2)}, u32[]{:S(2)}) collective-permute-start(bf16[1,32,256]{2,1,0:T(8,128)(2,1)S(1)} %collective-permute-done.12), channel_id=1, source_target_pairs={{1,0},{2,1},{3,2},{4,3},{5,4},{6,5},{7,6},{8,7},{9,8},{10,9},{11,1... | collective-permute-start | bytes 49160 | tf_op jit(solution)/shard_map/ppermute | solution.py:24
  41.7 0.5 collective-permute-done.6
  42.2 0.0 collective-permute-start.7
  42.9 0.3 collective-permute-done.13
  43.2 4.4 %collective-permute-start.14 = (bf16[1,32,256]{2,1,0:T(8,128)(2,1)S(1)}, bf16[1,32,256]{2,1,0:T(8,128)(2,1)S(1)}, u32[]{:S(2)}, u32[]{:S(2)}) collective-permute-start(bf16[1,32,256]{2,1,0:T(8,128)(2,1)S(1)} %collective-permute-done.13), channel_id=1, source_target_pairs={{1,0},{2,1},{3,2},{4,3},{5,4},{6,5},{7,6},{8,7},{9,8},{10,9},{11,1... | collective-permute-start | bytes 49160 | tf_op jit(solution)/shard_map/ppermute | solution.py:24
  47.6 0.5 collective-permute-done.7
  48.2 0.7 constant_dynamic-update-slice_fusion.7
  48.9 0.1 collective-permute-done.14
  49.0 0.6 gather_fusion
  49.6 0.2 fusion
  49.8 1.3 %collective-permute-start.15 = (bf16[1,32,512]{2,1,0:T(8,128)(2,1)S(1)}, bf16[1,32,512]{2,1,0:T(8,128)(2,1)S(1)}, u32[]{:S(2)}, u32[]{:S(2)}) collective-permute-start(bf16[1,32,512]{2,1,0:T(8,128)(2,1)S(1)} %get-tuple-element.28), channel_id=1, source_target_pairs={{0,1},{1,2},{2,3},{3,4},{4,5},{5,6},{6,7},{7,8},{8,9},{9,10},{10,1... | collective-permute-start | bytes 98312 | tf_op jit(solution)/shard_map/ppermute | solution.py:39
  51.1 1.3 %collective-permute-start.16 = (bf16[1,32,512]{2,1,0:T(8,128)(2,1)S(1)}, bf16[1,32,512]{2,1,0:T(8,128)(2,1)S(1)}, u32[]{:S(2)}, u32[]{:S(2)}) collective-permute-start(bf16[1,32,512]{2,1,0:T(8,128)(2,1)S(1)} %get-tuple-element.29), channel_id=1, source_target_pairs={{1,0},{2,1},{3,2},{4,3},{5,4},{6,5},{7,6},{8,7},{9,8},{10,9},{11,1... | collective-permute-start | bytes 98312 | tf_op jit(solution)/shard_map/ppermute | solution.py:41
  52.5 0.0 collective-permute-done.15
  52.5 1.7 %collective-permute-done.16 = bf16[1,32,512]{2,1,0:T(8,128)(2,1)S(1)} collective-permute-done((bf16[1,32,512]{2,1,0:T(8,128)(2,1)S(1)}, bf16[1,32,512]{2,1,0:T(8,128)(2,1)S(1)}, u32[]{:S(2)}, u32[]{:S(2)}) %collective-permute-start.16) | collective-permute-done | bytes 32800 | tf_op jit(solution)/shard_map/ppermute | solution.py:41
  54.2 0.1 pad_slice_fusion.45
  54.3 0.7 multiply_add_fusion.1
  55.0 0.0 copy-start.1
  55.0 0.7 multiply_add_fusion
  55.8 2.5 %fusion.152 = (f32[8,2,32,512]{3,2,1,0:T(8,128)S(1)}, bf16[8,2,32,512]{3,2,1,0:T(8,128)(2,1)S(1)}) fusion(f32[8]{0:T(128)S(1)} %copy-done.1, f32[8,2,32,512]{3,2,1,0:T(8,128)S(1)} %multiply_add_fusion.1, f32[8]{0:T(128)S(1)} %get-tuple-element.64, f32[8]{0:T(128)S(1)} %get-tuple-element.65, f32[8]{0:T(128)S(1)} %get-tuple-element.58, ...), kind=kLoop, calls=%fused_computation.279 | loop fusion | flops 7864320 | bytes 2627904 | tf_op jit(solution)/shard_map/convert_element_type | solution.py:66
  58.3 2.1 %collective-permute-start.17 = (bf16[8,1,32,512]{3,2,1,0:T(8,128)(2,1)S(1)}, bf16[8,1,32,512]{3,2,1,0:T(8,128)(2,1)S(1)}, u32[]{:S(2)}, u32[]{:S(2)}) collective-permute-start(bf16[8,1,32,512]{3,2,1,0:T(8,128)(2,1)S(1)} %get-tuple-element.15), channel_id=1, source_target_pairs={{0,1},{1,2},{2,3},{3,4},{4,5},{5,6},{6,7},{7,8},{8,9},{9,10},{10,1... | collective-permute-start | bytes 786440 | tf_op jit(solution)/shard_map/ppermute | solution.py:39
  60.4 1.3 %collective-permute-start.18 = (bf16[8,1,32,512]{3,2,1,0:T(8,128)(2,1)S(1)}, bf16[8,1,32,512]{3,2,1,0:T(8,128)(2,1)S(1)}, u32[]{:S(2)}, u32[]{:S(2)}) collective-permute-start(bf16[8,1,32,512]{3,2,1,0:T(8,128)(2,1)S(1)} %get-tuple-element.14), channel_id=1, source_target_pairs={{1,0},{2,1},{3,2},{4,3},{5,4},{6,5},{7,6},{8,7},{9,8},{10,9},{11,1... | collective-permute-start | bytes 786440 | tf_op jit(solution)/shard_map/ppermute | solution.py:41
  61.7 2.5 %fusion.154 = (f32[8,2,32,512]{3,2,1,0:T(8,128)S(1)}, bf16[8,2,32,512]{3,2,1,0:T(8,128)(2,1)S(1)}) fusion(f32[8]{0:T(128)S(1)} %copy-done.1, f32[8,2,32,512]{3,2,1,0:T(8,128)S(1)} %multiply_add_fusion, f32[8]{0:T(128)S(1)} %get-tuple-element.55, f32[8]{0:T(128)S(1)} %get-tuple-element.56, f32[8]{0:T(128)S(1)} %get-tuple-element.49, ...), kind=kLoop, calls=%fused_computation.280 | loop fusion | flops 7864320 | bytes 2627904 | tf_op jit(solution)/shard_map/convert_element_type | solution.py:66
  64.2 3.0 %collective-permute-start.19 = (bf16[8,1,32,512]{3,2,1,0:T(8,128)(2,1)S(1)}, bf16[8,1,32,512]{3,2,1,0:T(8,128)(2,1)S(1)}, u32[]{:S(2)}, u32[]{:S(2)}) collective-permute-start(bf16[8,1,32,512]{3,2,1,0:T(8,128)(2,1)S(1)} %get-tuple-element.19), channel_id=1, source_target_pairs={{0,1},{1,2},{2,3},{3,4},{4,5},{5,6},{6,7},{7,8},{8,9},{9,10},{10,1... | collective-permute-start | bytes 786440 | tf_op jit(solution)/shard_map/ppermute | solution.py:39
  67.2 1.5 %collective-permute-start.20 = (bf16[8,1,32,512]{3,2,1,0:T(8,128)(2,1)S(1)}, bf16[8,1,32,512]{3,2,1,0:T(8,128)(2,1)S(1)}, u32[]{:S(2)}, u32[]{:S(2)}) collective-permute-start(bf16[8,1,32,512]{3,2,1,0:T(8,128)(2,1)S(1)} %get-tuple-element.18), channel_id=1, source_target_pairs={{1,0},{2,1},{3,2},{4,3},{5,4},{6,5},{7,6},{8,7},{9,8},{10,9},{11,1... | collective-permute-start | bytes 786440 | tf_op jit(solution)/shard_map/ppermute | solution.py:41
  68.7 0.0 collective-permute-done.17
  68.7 0.0 collective-permute-done.18
  68.7 0.1 fusion.135
  68.9 1.6 %fusion.35 = f32[8,2,32,512]{3,2,1,0:T(8,128)S(1)} fusion(f32[8,2,32,512]{3,2,1,0:T(8,128)S(1)} %get-tuple-element.13, f32[8,2,32,512]{3,2,1,0:T(8,128)S(1)} %get-tuple-element.8, f32[8,2,32,512]{3,2,1,0:T(8,128)S(1)} %get-tuple-element.12, f32[8]{0:T(128)S(1)} %get-tuple-element.37, f32[8]{0:T(128)S(1)} %get-tuple-element.38, f32[8]{0:T(128)S(1)} %get-tuple-element.31, ...), kind=kLoop, calls=%fused_computation.81 | loop fusion | flops 4456448 | bytes 4194592 | tf_op jit(solution)/shard_map/add | solution.py:68
  70.5 2.4 %fusion.132 = f32[2,32,512]{2,1,0:T(8,128)S(1)} fusion(f32[8,2,32,512]{3,2,1,0:T(8,128)S(1)} %fusion.35, f32[8]{0:T(128)S(1)} %get-tuple-element.46, f32[8]{0:T(128)S(1)} %get-tuple-element.47, f32[8]{0:T(128)S(1)} %get-tuple-element.40, f32[8]{0:T(128)S(1)} %get-tuple-element.41, f32[8]{0:T(128)S(1)} %get-tuple-element.42, f32[8]{0:T(128)S(1)} %get-tuple-element.43, ...), kind=kLoop, calls=%fused_computation.180 | loop fusion | flops 7045120 | bytes 1186080 | tf_op jit(solution)/shard_map/reduce_sum | solution.py:100
  72.9 0.0 collective-permute-done.19
  72.9 0.0 collective-permute-done.20
  72.9 0.1 fusion.133
  73.1 1.6 %fusion.99 = f32[8,2,32,512]{3,2,1,0:T(8,128)S(1)} fusion(f32[8,2,32,512]{3,2,1,0:T(8,128)S(1)} %get-tuple-element.17, f32[8,2,32,512]{3,2,1,0:T(8,128)S(1)} %get-tuple-element.10, f32[8,2,32,512]{3,2,1,0:T(8,128)S(1)} %get-tuple-element.16, f32[8]{0:T(128)S(1)} %get-tuple-element.46, f32[8]{0:T(128)S(1)} %get-tuple-element.47, f32[8]{0:T(128)S(1)} %get-tuple-element.40, ...), kind=kLoop, calls=%fused_computation.145 | loop fusion | flops 4456448 | bytes 4194592 | tf_op jit(solution)/shard_map/add | solution.py:68
  74.7 2.4 %fusion.131 = f32[2,32,512]{2,1,0:T(8,128)S(1)} fusion(f32[8,2,32,512]{3,2,1,0:T(8,128)S(1)} %fusion.99, f32[8]{0:T(128)S(1)} %get-tuple-element.37, f32[8]{0:T(128)S(1)} %get-tuple-element.38, f32[8]{0:T(128)S(1)} %get-tuple-element.31, f32[8]{0:T(128)S(1)} %get-tuple-element.32, f32[8]{0:T(128)S(1)} %get-tuple-element.33, f32[8]{0:T(128)S(1)} %get-tuple-element.34, ...), kind=kLoop, calls=%fused_computation.179 | loop fusion | flops 7045120 | bytes 1186080 | tf_op jit(solution)/shard_map/reduce_sum | solution.py:100
  77.1 0.1 fusion.151
  77.2 37.1 %pmax.7 = f32[512]{0:T(512)S(1)} all-reduce(f32[512]{0:T(512)S(1)} %get-tuple-element.5), channel_id=1, replica_groups=mesh['groups'=2,'arow'=16] {'arow'}, use_global_device_ids=true, to_apply=%region_3.4 | all-reduce | flops 512 | bytes 4096 | tf_op jit(solution)/shard_map/pmax | solution.py:129
  114.4 0.7 fusion.137
  (30 shorter events, 0.2 us)
Async XLA Ops:
  0.0 49.6 %copy-start = (bf16[2,32,256]{2,1,0:T(8,128)(2,1)S(1)}, bf16[2,32,256]{2,1,0:T(8,128)(2,1)}, u32[]{:S(2)}) copy-start(bf16[2,32,256]{2,1,0:T(8,128)(2,1)} %param.8) | copy-start | bytes 98308
  0.0 7.0 %collective-permute-start = (bf16[1,32,256]{2,1,0:T(8,128)(2,1)}, bf16[1,32,256]{2,1,0:T(8,128)(2,1)S(1)}, u32[]{:S(2)}, u32[]{:S(2)}) collective-permute-start(bf16[1,32,256]{2,1,0:T(8,128)(2,1)} %param.9), channel_id=1, source_target_pairs={{0,1},{1,2},{2,3},{3,4},{4,5},{5,6},{6,7},{7,8},{8,9},{9,10},{10,1... | collective-permute-start | bytes 49160 | tf_op jit(solution)/shard_map/ppermute | solution.py:22
  0.5 13.3 %collective-permute-start.8 = (bf16[1,32,256]{2,1,0:T(8,128)(2,1)}, bf16[1,32,256]{2,1,0:T(8,128)(2,1)S(1)}, u32[]{:S(2)}, u32[]{:S(2)}) collective-permute-start(bf16[1,32,256]{2,1,0:T(8,128)(2,1)} %param.9), channel_id=1, source_target_pairs={{1,0},{2,1},{3,2},{4,3},{5,4},{6,5},{7,6},{8,7},{9,8},{10,9},{11,1... | collective-permute-start | bytes 49160 | tf_op jit(solution)/shard_map/ppermute | solution.py:24
  7.1 5.9 %collective-permute-start.1 = (bf16[1,32,256]{2,1,0:T(8,128)(2,1)S(1)}, bf16[1,32,256]{2,1,0:T(8,128)(2,1)S(1)}, u32[]{:S(2)}, u32[]{:S(2)}) collective-permute-start(bf16[1,32,256]{2,1,0:T(8,128)(2,1)S(1)} %collective-permute-done), channel_id=1, source_target_pairs={{0,1},{1,2},{2,3},{3,4},{4,5},{5,6},{6,7},{7,8},{8,9},{9,10},{10,1... | collective-permute-start | bytes 49160 | tf_op jit(solution)/shard_map/ppermute | solution.py:22
  12.9 5.9 %collective-permute-start.2 = (bf16[1,32,256]{2,1,0:T(8,128)(2,1)S(1)}, bf16[1,32,256]{2,1,0:T(8,128)(2,1)S(1)}, u32[]{:S(2)}, u32[]{:S(2)}) collective-permute-start(bf16[1,32,256]{2,1,0:T(8,128)(2,1)S(1)} %collective-permute-done.1), channel_id=1, source_target_pairs={{0,1},{1,2},{2,3},{3,4},{4,5},{5,6},{6,7},{7,8},{8,9},{9,10},{10,1... | collective-permute-start | bytes 49160 | tf_op jit(solution)/shard_map/ppermute | solution.py:22
  13.8 5.9 %collective-permute-start.9 = (bf16[1,32,256]{2,1,0:T(8,128)(2,1)S(1)}, bf16[1,32,256]{2,1,0:T(8,128)(2,1)S(1)}, u32[]{:S(2)}, u32[]{:S(2)}) collective-permute-start(bf16[1,32,256]{2,1,0:T(8,128)(2,1)S(1)} %collective-permute-done.8), channel_id=1, source_target_pairs={{1,0},{2,1},{3,2},{4,3},{5,4},{6,5},{7,6},{8,7},{9,8},{10,9},{11,1... | collective-permute-start | bytes 49160 | tf_op jit(solution)/shard_map/ppermute | solution.py:24
  18.8 5.9 %collective-permute-start.3 = (bf16[1,32,256]{2,1,0:T(8,128)(2,1)S(1)}, bf16[1,32,256]{2,1,0:T(8,128)(2,1)S(1)}, u32[]{:S(2)}, u32[]{:S(2)}) collective-permute-start(bf16[1,32,256]{2,1,0:T(8,128)(2,1)S(1)} %collective-permute-done.2), channel_id=1, source_target_pairs={{0,1},{1,2},{2,3},{3,4},{4,5},{5,6},{6,7},{7,8},{8,9},{9,10},{10,1... | collective-permute-start | bytes 49160 | tf_op jit(solution)/shard_map/ppermute | solution.py:22
  19.7 5.9 %collective-permute-start.10 = (bf16[1,32,256]{2,1,0:T(8,128)(2,1)S(1)}, bf16[1,32,256]{2,1,0:T(8,128)(2,1)S(1)}, u32[]{:S(2)}, u32[]{:S(2)}) collective-permute-start(bf16[1,32,256]{2,1,0:T(8,128)(2,1)S(1)} %collective-permute-done.9), channel_id=1, source_target_pairs={{1,0},{2,1},{3,2},{4,3},{5,4},{6,5},{7,6},{8,7},{9,8},{10,9},{11,1... | collective-permute-start | bytes 49160 | tf_op jit(solution)/shard_map/ppermute | solution.py:24
  24.6 5.9 %collective-permute-start.4 = (bf16[1,32,256]{2,1,0:T(8,128)(2,1)S(1)}, bf16[1,32,256]{2,1,0:T(8,128)(2,1)S(1)}, u32[]{:S(2)}, u32[]{:S(2)}) collective-permute-start(bf16[1,32,256]{2,1,0:T(8,128)(2,1)S(1)} %collective-permute-done.3), channel_id=1, source_target_pairs={{0,1},{1,2},{2,3},{3,4},{4,5},{5,6},{6,7},{7,8},{8,9},{9,10},{10,1... | collective-permute-start | bytes 49160 | tf_op jit(solution)/shard_map/ppermute | solution.py:22
  25.6 5.9 %collective-permute-start.11 = (bf16[1,32,256]{2,1,0:T(8,128)(2,1)S(1)}, bf16[1,32,256]{2,1,0:T(8,128)(2,1)S(1)}, u32[]{:S(2)}, u32[]{:S(2)}) collective-permute-start(bf16[1,32,256]{2,1,0:T(8,128)(2,1)S(1)} %collective-permute-done.10), channel_id=1, source_target_pairs={{1,0},{2,1},{3,2},{4,3},{5,4},{6,5},{7,6},{8,7},{9,8},{10,9},{11,1... | collective-permute-start | bytes 49160 | tf_op jit(solution)/shard_map/ppermute | solution.py:24
  30.5 5.9 %collective-permute-start.5 = (bf16[1,32,256]{2,1,0:T(8,128)(2,1)S(1)}, bf16[1,32,256]{2,1,0:T(8,128)(2,1)S(1)}, u32[]{:S(2)}, u32[]{:S(2)}) collective-permute-start(bf16[1,32,256]{2,1,0:T(8,128)(2,1)S(1)} %collective-permute-done.4), channel_id=1, source_target_pairs={{0,1},{1,2},{2,3},{3,4},{4,5},{5,6},{6,7},{7,8},{8,9},{9,10},{10,1... | collective-permute-start | bytes 49160 | tf_op jit(solution)/shard_map/ppermute | solution.py:22
  31.4 5.9 %collective-permute-start.12 = (bf16[1,32,256]{2,1,0:T(8,128)(2,1)S(1)}, bf16[1,32,256]{2,1,0:T(8,128)(2,1)S(1)}, u32[]{:S(2)}, u32[]{:S(2)}) collective-permute-start(bf16[1,32,256]{2,1,0:T(8,128)(2,1)S(1)} %collective-permute-done.11), channel_id=1, source_target_pairs={{1,0},{2,1},{3,2},{4,3},{5,4},{6,5},{7,6},{8,7},{9,8},{10,9},{11,1... | collective-permute-start | bytes 49160 | tf_op jit(solution)/shard_map/ppermute | solution.py:24
  36.4 5.9 %collective-permute-start.6 = (bf16[1,32,256]{2,1,0:T(8,128)(2,1)S(1)}, bf16[1,32,256]{2,1,0:T(8,128)(2,1)S(1)}, u32[]{:S(2)}, u32[]{:S(2)}) collective-permute-start(bf16[1,32,256]{2,1,0:T(8,128)(2,1)S(1)} %collective-permute-done.5), channel_id=1, source_target_pairs={{0,1},{1,2},{2,3},{3,4},{4,5},{5,6},{6,7},{7,8},{8,9},{9,10},{10,1... | collective-permute-start | bytes 49160 | tf_op jit(solution)/shard_map/ppermute | solution.py:22
  37.3 5.9 %collective-permute-start.13 = (bf16[1,32,256]{2,1,0:T(8,128)(2,1)S(1)}, bf16[1,32,256]{2,1,0:T(8,128)(2,1)S(1)}, u32[]{:S(2)}, u32[]{:S(2)}) collective-permute-start(bf16[1,32,256]{2,1,0:T(8,128)(2,1)S(1)} %collective-permute-done.12), channel_id=1, source_target_pairs={{1,0},{2,1},{3,2},{4,3},{5,4},{6,5},{7,6},{8,7},{9,8},{10,9},{11,1... | collective-permute-start | bytes 49160 | tf_op jit(solution)/shard_map/ppermute | solution.py:24
  42.2 5.9 %collective-permute-start.7 = (bf16[1,32,256]{2,1,0:T(8,128)(2,1)S(1)}, bf16[1,32,256]{2,1,0:T(8,128)(2,1)S(1)}, u32[]{:S(2)}, u32[]{:S(2)}) collective-permute-start(bf16[1,32,256]{2,1,0:T(8,128)(2,1)S(1)} %collective-permute-done.6), channel_id=1, source_target_pairs={{0,1},{1,2},{2,3},{3,4},{4,5},{5,6},{6,7},{7,8},{8,9},{9,10},{10,1... | collective-permute-start | bytes 49160 | tf_op jit(solution)/shard_map/ppermute | solution.py:22
  43.2 5.9 %collective-permute-start.14 = (bf16[1,32,256]{2,1,0:T(8,128)(2,1)S(1)}, bf16[1,32,256]{2,1,0:T(8,128)(2,1)S(1)}, u32[]{:S(2)}, u32[]{:S(2)}) collective-permute-start(bf16[1,32,256]{2,1,0:T(8,128)(2,1)S(1)} %collective-permute-done.13), channel_id=1, source_target_pairs={{1,0},{2,1},{3,2},{4,3},{5,4},{6,5},{7,6},{8,7},{9,8},{10,9},{11,1... | collective-permute-start | bytes 49160 | tf_op jit(solution)/shard_map/ppermute | solution.py:24
  49.8 2.7 %collective-permute-start.15 = (bf16[1,32,512]{2,1,0:T(8,128)(2,1)S(1)}, bf16[1,32,512]{2,1,0:T(8,128)(2,1)S(1)}, u32[]{:S(2)}, u32[]{:S(2)}) collective-permute-start(bf16[1,32,512]{2,1,0:T(8,128)(2,1)S(1)} %get-tuple-element.28), channel_id=1, source_target_pairs={{0,1},{1,2},{2,3},{3,4},{4,5},{5,6},{6,7},{7,8},{8,9},{9,10},{10,1... | collective-permute-start | bytes 98312 | tf_op jit(solution)/shard_map/ppermute | solution.py:39
  51.1 3.1 %collective-permute-start.16 = (bf16[1,32,512]{2,1,0:T(8,128)(2,1)S(1)}, bf16[1,32,512]{2,1,0:T(8,128)(2,1)S(1)}, u32[]{:S(2)}, u32[]{:S(2)}) collective-permute-start(bf16[1,32,512]{2,1,0:T(8,128)(2,1)S(1)} %get-tuple-element.29), channel_id=1, source_target_pairs={{1,0},{2,1},{3,2},{4,3},{5,4},{6,5},{7,6},{8,7},{9,8},{10,9},{11,1... | collective-permute-start | bytes 98312 | tf_op jit(solution)/shard_map/ppermute | solution.py:41
  55.0 0.7 copy-start.1
  58.3 10.4 %collective-permute-start.17 = (bf16[8,1,32,512]{3,2,1,0:T(8,128)(2,1)S(1)}, bf16[8,1,32,512]{3,2,1,0:T(8,128)(2,1)S(1)}, u32[]{:S(2)}, u32[]{:S(2)}) collective-permute-start(bf16[8,1,32,512]{3,2,1,0:T(8,128)(2,1)S(1)} %get-tuple-element.15), channel_id=1, source_target_pairs={{0,1},{1,2},{2,3},{3,4},{4,5},{5,6},{6,7},{7,8},{8,9},{9,10},{10,1... | collective-permute-start | bytes 786440 | tf_op jit(solution)/shard_map/ppermute | solution.py:39
  60.4 8.4 %collective-permute-start.18 = (bf16[8,1,32,512]{3,2,1,0:T(8,128)(2,1)S(1)}, bf16[8,1,32,512]{3,2,1,0:T(8,128)(2,1)S(1)}, u32[]{:S(2)}, u32[]{:S(2)}) collective-permute-start(bf16[8,1,32,512]{3,2,1,0:T(8,128)(2,1)S(1)} %get-tuple-element.14), channel_id=1, source_target_pairs={{1,0},{2,1},{3,2},{4,3},{5,4},{6,5},{7,6},{8,7},{9,8},{10,9},{11,1... | collective-permute-start | bytes 786440 | tf_op jit(solution)/shard_map/ppermute | solution.py:41
  64.2 8.7 %collective-permute-start.19 = (bf16[8,1,32,512]{3,2,1,0:T(8,128)(2,1)S(1)}, bf16[8,1,32,512]{3,2,1,0:T(8,128)(2,1)S(1)}, u32[]{:S(2)}, u32[]{:S(2)}) collective-permute-start(bf16[8,1,32,512]{3,2,1,0:T(8,128)(2,1)S(1)} %get-tuple-element.19), channel_id=1, source_target_pairs={{0,1},{1,2},{2,3},{3,4},{4,5},{5,6},{6,7},{7,8},{8,9},{9,10},{10,1... | collective-permute-start | bytes 786440 | tf_op jit(solution)/shard_map/ppermute | solution.py:39
  67.2 5.7 %collective-permute-start.20 = (bf16[8,1,32,512]{3,2,1,0:T(8,128)(2,1)S(1)}, bf16[8,1,32,512]{3,2,1,0:T(8,128)(2,1)S(1)}, u32[]{:S(2)}, u32[]{:S(2)}) collective-permute-start(bf16[8,1,32,512]{3,2,1,0:T(8,128)(2,1)S(1)} %get-tuple-element.18), channel_id=1, source_target_pairs={{1,0},{2,1},{3,2},{4,3},{5,4},{6,5},{7,6},{8,7},{9,8},{10,9},{11,1... | collective-permute-start | bytes 786440 | tf_op jit(solution)/shard_map/ppermute | solution.py:41
